TPU v7x, 512 devices: a whole 4x8x8 slice. The times are simulated.
512 devices in a mesh: brick: 64 (over z, y), blk: 8 (over x, core).
Axes of the slice: x: 4, y: 8, z: 8, core: 2. Of those that a mesh axis runs over, the one named last changes fastest.
Arguments:
- parameters: float32 [4, 65536], P(None, ('brick', 'blk')), may hold values from -0.4 to 3, as said below
- sersic: float32 [65536], P(('brick', 'blk')), may hold values from 1 to 4
- psf_width: float32 [65536], P(('brick', 'blk')), may hold values from 0.8 to 2
- point_flag: int32 [65536], P(('brick', 'blk')), may hold values 0 or 1
- owner_brick: int32 [65536, 1], P(('brick', 'blk')), may hold values from 0 to 63; in each aligned block of 128 rows (0 to 127, 128 to 255, ...) at most 4 rows name the same one
- cell_index: int32 [65536], P(('brick', 'blk')), may hold values from 0 to 31
- exposure: float32 [16384, 1024], P(('brick', 'blk')), may hold values from -120 to 120
- inv_noise: float32 [16384], P(('brick', 'blk')), may hold values from 0.5 to 2
Outputs:
- updated: float32 [4, 65536], P(None, ('brick', 'blk'))
Inputs may be any that keep to these rules, and one draw needn't show every extreme that they name: `parameters`: row 0 is a flux from 0.5 to 3, rows 1 and 2 the centre's offsets within 0.4 pixels, row 3 the log radius from ln 1.5 to ln 6. `owner_brick`: the sources of one device name one brick at most 4 times.
All inputs are finite; a program needn't handle non-finite values. No bound on the sum of `point_flag` on one device may be relied on, other than what follows from the above.
Results may differ from a plain program's by a relative error of at most 0.0003.
Values sent between devices are 32-bit elements; how exact they have to be, the bound alone decides.
A program may use at most 64 MiB of HBM per device.

v0:
```python
import functools
import math

import jax
import jax.numpy as jnp
from jax import lax
from jax.experimental import pallas as pl
from jax.experimental.pallas import tpu as pltpu
from jax.sharding import PartitionSpec as P

TILE = 32
PIXELS = TILE * TILE
HALF = TILE // 2
PITCH = TILE + 1
LINES = 1096
SERIES = 96
CAP = 4
VALS = 32
BACK = 8
SIDE = 8
LANES = 128
ZERO_POINT = 30.0
BASE_DAMPING = 0.1
MISFIT_SCALE = 0.05
HIGHEST = lax.Precision.HIGHEST
MESH = pl.DeviceIdType.MESH
F32 = jnp.float32
BF16 = jnp.bfloat16

CX, CY, C1, C0, LN, INVN, ITV, NORM, SLOPE, CELL, WEIGHT = range(11)


def peer_offsets():
    return [(z, y) for z in sorted(range(SIDE), key=lambda step: (min(step, SIDE - step), step)) for y in range(SIDE)]


def dot(a, b, ca=1, cb=0):
    return lax.dot_general(
        a, b, (((ca,), (cb,)), ((), ())), precision=HIGHEST, preferred_element_type=F32
    )


def series(shape_value, cutoff):
    chain = SERIES // 8
    at = lax.broadcasted_iota(jnp.int32, (8, LANES), 0) * chain
    total = jnp.zeros((8, LANES), F32)
    product = jnp.ones((8, LANES), F32)
    for step in reversed(range(chain)):
        k = at + (step + 1)
        ratio = cutoff / (shape_value + k.astype(F32))
        live = k < SERIES
        total = jnp.where(live, ratio * (1.0 + total), 0.0)
        product = jnp.where(live, product * ratio, product)
    whole = total[7:8]
    last = product[7:8]
    for j in reversed(range(7)):
        whole = total[j : j + 1] + product[j : j + 1] * whole
        last = last * product[j : j + 1]
    return 1.0 + whole, last


def source_rows(values, sersic, psf_width, point, cell):
    flux, shift_x, shift_y, log_radius = (values[k : k + 1] for k in range(4))
    inverse_index = 1.0 / sersic
    bfactor = 2.0 * sersic - 1.0 / 3.0 + 4.0 / (405.0 * sersic)
    cutoff = bfactor * jnp.exp((math.log(0.5 * TILE) - log_radius) * inverse_index)
    total, last = series(2.0 * sersic, cutoff)
    log_norm = math.log(math.pi * 0.25 * TILE * TILE) - cutoff + jnp.log(total)
    slope = 2.0 - (2.0 * sersic - cutoff * last) * inverse_index / total
    inv_two_var = 0.5 / (psf_width * psf_width)
    norm_psf = 1.0 / (math.sqrt(2.0 * math.pi) * psf_width)
    is_point = point == 1
    log_itv = jnp.log(inv_two_var)
    rows = [None] * VALS
    rows[CX] = shift_x
    rows[CY] = shift_y
    rows[C1] = jnp.where(is_point, 1.0, 0.5 * inverse_index)
    rows[C0] = jnp.where(is_point, log_itv, jnp.log(bfactor) - log_radius * inverse_index)
    rows[LN] = jnp.where(is_point, math.log(math.pi) - log_itv, log_norm) - jnp.log(ZERO_POINT * flux)
    rows[INVN] = jnp.where(is_point, 2.0, inverse_index)
    rows[ITV] = jnp.where(is_point, 1.0e4, inv_two_var)
    rows[NORM] = jnp.where(is_point, 1.0, norm_psf)
    rows[SLOPE] = slope
    rows[CELL] = (cell + 1).astype(F32)
    zero = jnp.zeros_like(flux)
    return jnp.concatenate([zero if row is None else row for row in rows], axis=0)


def split(x):
    high = x.astype(BF16)
    return high, (x - high.astype(F32)).astype(BF16)


def product(a, b, cb=0):
    return lax.dot_general(a, b, (((1,), (cb,)), ((), ())), preferred_element_type=F32)


def blur_coefficients(row, taps, spread, coef, at):
    apart = lax.broadcasted_iota(jnp.int32, (TILE, LANES), 0).astype(F32)
    taps[...] = jnp.exp(-(apart * apart) * row(ITV)) * (0.5 * row(NORM))
    for d in range(TILE):
        value = jnp.broadcast_to(taps[d : d + 1, :], (8, LANES))
        spread[TILE - 1 + d] = value
        spread[TILE - 1 - d] = value
    for q in range(HALF):
        near = spread[TILE - 1 - q : TILE - 1 - q + HALF]
        far = spread[q : q + HALF]
        coef[at, 0, q] = near + far
        coef[at, 1, q] = near - far


def blur_lines(load, store, coef, at, parts, even_acc):
    for q in range(HALF):
        low, high = load(q), load(TILE - 1 - q)
        parts[0, q] = low + high
        parts[1, q] = low - high
    for parity in range(2):
        for group in range(2):
            span = slice(group * 8, group * 8 + 8)
            acc = None
            for q in range(HALF):
                term = coef[at, parity, q, span][None] * parts[parity, q][:, None]
                acc = term if acc is None else acc + term
            if parity == 0:
                even_acc[group] = acc
            else:
                even = even_acc[group]
                for k in range(8):
                    store(group * 8 + k, even[:, k] + acc[:, k])
                    store(TILE - 1 - group * 8 - k, even[:, k] - acc[:, k])


def blur(first, count, at_of, src, mid, dst, coef, parts, even_acc):
    def along_major(step, carry):
        image, start = first + step // 2, (step % 2) * 16

        def load(q):
            return src[image, pl.ds(q * PITCH + start, 16), :].reshape(2, 8, LANES)

        def store(q, value):
            mid[image, pl.ds(q * PITCH + start, 16), :] = value.reshape(16, LANES)

        blur_lines(load, store, coef, at_of(image), parts, even_acc)
        return carry

    def along_minor(step, carry):
        image, start = first + step // 2, (step % 2) * 16

        def load(p):
            return mid[image, pl.ds(start * PITCH + p, 16, stride=PITCH), :].reshape(2, 8, LANES)

        def store(p, value):
            dst[image, pl.ds(p * PITCH + start, 16), :] = value.reshape(16, LANES)

        blur_lines(load, store, coef, at_of(image), parts, even_acc)
        return carry

    lax.fori_loop(0, 2 * count, along_major, 0)
    lax.fori_loop(0, 2 * count, along_minor, 0)


def offsets(row, dy_ref, at):
    t_p = lax.broadcasted_iota(jnp.int32, (TILE, LANES), 0).astype(F32) + (0.5 - 0.5 * TILE)
    dy = t_p - row(CY)
    dy_ref[at, 0] = dy
    dy_ref[at, 1] = dy * dy


def column(q, row):
    return q.astype(F32) + (0.5 - 0.5 * TILE) - row(CX)


def images(q, row, dy_ref, at):
    dx = column(q, row)
    radius_sq = dy_ref[at, 1] + dx * dx
    power = jnp.exp(row(C1) * jnp.log(radius_sq) + row(C0))
    image = jnp.exp(-power - row(LN))
    over = image * (power * row(INVN)) / radius_sq
    return dx, radius_sq, image, over


def damped_solve(curvature, gradient, damping):
    system = [[curvature[first][second] for second in range(4)] for first in range(4)]
    for first in range(4):
        system[first][first] = system[first][first] + damping * (1.0 + curvature[first][first])
    factor = [[None for second in range(4)] for first in range(4)]
    for column in range(4):
        pivot = system[column][column]
        for inner in range(column):
            pivot = pivot - factor[column][inner] * factor[column][inner]
        pivot = jnp.sqrt(pivot)
        factor[column][column] = pivot
        for lower_row in range(column + 1, 4):
            entry = system[lower_row][column]
            for inner in range(column):
                entry = entry - factor[lower_row][inner] * factor[column][inner]
            factor[lower_row][column] = entry / pivot
    forward = []
    for row_at in range(4):
        entry = gradient[row_at]
        for inner in range(row_at):
            entry = entry - factor[row_at][inner] * forward[inner]
        forward.append(entry / factor[row_at][row_at])
    solved = [None, None, None, None]
    for row_at in reversed(range(4)):
        entry = forward[row_at]
        for inner in range(row_at + 1, 4):
            entry = entry - factor[inner][row_at] * solved[inner]
        solved[row_at] = entry / factor[row_at][row_at]
    return solved


def kernel(
    blocks, pixel_total, remote,
    values_hbm, sersic_hbm, psf_hbm, flag_hbm, owner_hbm, cell_hbm, exposure_hbm, noise_hbm,
    out_ref,
    values_ref, sersic_ref, psf_ref, flag_ref, owner_ref, cell_ref, exposure_ref, noise_ref,
    rows_ref, hits_ref, rank_ref, slots_ref, gram_ref, taps, spread, coef, parts, even_acc, dy_ref,
    img_a, img_b, img_c, img_d, img_e, exposure_t, weighted_ref,
    out_rows, mid_rows, in_rows, out_sums, in_sums, chi_out, chi_in,
    input_sem, send_sem, mid_sem, pass_sem, near_sem, far_sem, back_send_sem, back_sem, chi_send_sem, chi_sem,
):
    inputs = [
        pltpu.make_async_copy(source, target, input_sem.at[k])
        for k, (source, target) in enumerate(
            (
                (values_hbm, values_ref),
                (sersic_hbm, sersic_ref),
                (psf_hbm, psf_ref),
                (flag_hbm, flag_ref),
                (owner_hbm, owner_ref),
                (cell_hbm, cell_ref),
                (exposure_hbm, exposure_ref),
                (noise_hbm, noise_ref),
            )
        )
    ]
    for copy in inputs:
        copy.start()
    offsets_of = peer_offsets()
    peers = len(offsets_of)
    near = peers // 2
    if remote:
        me = lax.axis_index("brick")
        lane = lax.axis_index("blk")
        barrier = pltpu.get_barrier_semaphore()
        my_z, my_y = me // SIDE, me % SIDE
        plus_z = [((my_z + k) % SIDE) * SIDE for k in range(SIDE)]
        plus_y = [(my_y + k) % SIDE for k in range(SIDE)]

        def ahead(j):
            return plus_z[offsets_of[j][0]] + plus_y[offsets_of[j][1]]

        def behind(j):
            return plus_z[-offsets_of[j][0] % SIDE] + plus_y[-offsets_of[j][1] % SIDE]

        def around(k):
            return jnp.where(lane + k >= blocks, lane + k - blocks, lane + k)

        for k in reversed(range(1, SIDE)):
            pl.semaphore_signal(barrier, inc=1, device_id={"brick": ahead(k)}, device_id_type=MESH)
            pl.semaphore_signal(barrier, inc=1, device_id={"brick": ahead(k * SIDE)}, device_id_type=MESH)
        for k in range(1, blocks):
            pl.semaphore_signal(barrier, inc=1, device_id={"blk": around(k)}, device_id_type=MESH)
    else:
        my_z, my_y = 0, 0
    for copy in inputs[:6]:
        copy.wait()

    rows = source_rows(values_ref[...], sersic_ref[...], psf_ref[...], flag_ref[...], cell_ref[...])
    rows_ref[...] = rows
    owner = owner_ref[...].astype(F32)
    owner_all = jnp.broadcast_to(owner, (LANES, LANES))
    earlier = lax.broadcasted_iota(jnp.int32, (LANES, LANES), 0) < lax.broadcasted_iota(jnp.int32, (LANES, LANES), 1)
    same = jnp.where((owner_all.T == owner_all) & earlier, 1.0, 0.0)
    rank = jnp.sum(same, axis=0, keepdims=True)
    rank_ref[...] = rank
    place = owner_ref[...]
    ahead_of_me = (((place >> 3) - my_z) & (SIDE - 1)) * SIDE + (((place & (SIDE - 1)) - my_y) & (SIDE - 1))
    for j, (z, y) in enumerate(offsets_of):
        hits_ref[j : j + 1, :] = jnp.where(ahead_of_me == z * SIDE + y, 1.0, 0.0)
    by_rank = jnp.concatenate([jnp.where(rank == float(r), rows, 0.0) for r in range(CAP)], axis=0)
    out_rows[:, :, 0, :] = dot(hits_ref[...], by_rank, 1, 1).reshape(SIDE, SIDE, LANES)

    def row(k):
        return rows_ref[k : k + 1, :]

    blur_coefficients(row, taps, spread, coef, 2)
    offsets(row, dy_ref, 2)

    def own_images(q, carry):
        dx, radius_sq, image, over = images(q, row, dy_ref, 2)
        at = pl.ds(q * PITCH, TILE)
        img_d[0, at, :] = image
        img_d[1, at, :] = over * dx
        img_d[2, at, :] = over * dy_ref[2, 0]
        img_d[3, at, :] = over * radius_sq - row(SLOPE) * image
        return carry

    lax.fori_loop(0, TILE, own_images, 0, unroll=4)

    def own_blur(first, count):
        blur(first, count, lambda image: 2, img_d, img_e, img_d, coef, parts, even_acc)

    if remote:
        pl.semaphore_wait(barrier, 2 * (SIDE - 1) + blocks - 1)

        def send(source, target, to, sent, landed):
            pltpu.make_async_remote_copy(
                src_ref=source, dst_ref=target, send_sem=sent, recv_sem=landed,
                device_id={"brick": to}, device_id_type=MESH,
            ).start()

        def await_rows(ref, count, sem):
            pltpu.make_async_copy(ref.at[0:count], ref.at[0:count], sem).wait()

        for k in range(1, SIDE):
            send(out_rows.at[:, k], mid_rows.at[:, k], ahead(k), send_sem.at[0], mid_sem.at[0])
    mid_rows[:, 0] = out_rows[:, 0]
    own_blur(0, 2)
    if remote:
        await_rows(mid_rows, SIDE - 1, mid_sem.at[0])
        for k in reversed(range(1, SIDE)):
            landed = (near_sem if k < SIDE // 2 else far_sem).at[0]
            send(mid_rows.at[k], in_rows.at[k], ahead(k * SIDE), pass_sem.at[0], landed)
        in_rows[0] = mid_rows[0]
    else:
        in_rows[...] = out_rows[...]

    own_blur(2, 1)
    for copy in inputs[6:]:
        copy.wait()
    cells = exposure_ref.shape[0]
    for k in range(PIXELS // LANES):
        part = exposure_ref[:, k * LANES : (k + 1) * LANES].T
        exposure_t[k * LANES : (k + 1) * LANES, :] = jnp.concatenate([part, part], axis=1)

    noise = noise_ref[...]
    weights = noise * noise
    cells_at = lax.broadcasted_iota(jnp.int32, (cells, LANES), 0).astype(F32) + 1.0
    picks = []

    def slot_rows(half):
        return lambda k: slots_ref[half, k : k + 1, :]

    def render(half):
        received = in_rows[half * SIDE // 2 : (half + 1) * SIDE // 2, :, 0, :].reshape(near, LANES)
        turned = [received] + [pltpu.roll(received, LANES - r * VALS, 1) for r in range(1, CAP)]
        slots_ref[half] = jnp.concatenate(turned, axis=0).T[:VALS]
        slot = slot_rows(half)
        blur_coefficients(slot, taps, spread, coef, half)
        offsets(slot, dy_ref, half)

        def slot_images(q, carry):
            dx, radius_sq, image, over = images(q, slot, dy_ref, half)
            at = pl.ds(q * PITCH, TILE)
            img_a[half, at, :] = image
            img_b[half, at, :] = over
            return carry

        lax.fori_loop(0, TILE, slot_images, 0, unroll=8)
        blur(half, 1, lambda image: half, img_a, img_e, img_c, coef, parts, even_acc)
        chosen = jnp.where(cells_at == slot(CELL), 1.0, 0.0)
        picks.append(chosen)
        slots_ref[half, WEIGHT : WEIGHT + 1, :] = dot(jnp.broadcast_to(weights, (8, cells)), chosen)[0:1]

    def lines_of(half, t):
        lines = [img_c[half, pl.ds((t * 8 + k) * PITCH, TILE), :] for k in range(8)]
        pick = jnp.concatenate([picks[half], picks[half]], axis=0).astype(BF16)
        tiles = jnp.concatenate(split(jnp.concatenate(lines, axis=0)), axis=1)
        return product(tiles, jnp.concatenate([pick, pick], axis=1), 1)

    def subtract_near(t, carry):
        at = pl.ds(pl.multiple_of(t * 8 * TILE, 8 * TILE), 8 * TILE)
        exposure_t[at, :] = exposure_t[at, :] - lines_of(0, t)
        return carry

    if remote:
        await_rows(in_rows, SIDE // 2 - 1, near_sem.at[0])
    render(0)
    lax.fori_loop(0, 4, subtract_near, 0, unroll=2)
    if remote:
        await_rows(in_rows, SIDE // 2, far_sem.at[0])
    render(1)
    weights_twice = jnp.concatenate([weights, weights], axis=1)
    is_high = lax.broadcasted_iota(jnp.int32, (1, 2 * cells), 1) < cells

    def residual(t, chi):
        at = pl.ds(pl.multiple_of(t * 8 * TILE, 8 * TILE), 8 * TILE)
        misfit = exposure_t[at, :] - lines_of(1, t)
        weighted = weights_twice * misfit
        high = weighted.astype(BF16).astype(F32)
        weighted_ref[at, :] = jnp.where(is_high, high, weighted - high).astype(BF16)
        return chi + jnp.sum((weighted * misfit).reshape(TILE, 8, 2 * cells), axis=0)

    chi = lax.fori_loop(0, 4, residual, jnp.zeros((8, 2 * cells), F32), unroll=2)
    chi = jnp.sum(chi, axis=0, keepdims=True)[:, :cells]
    chi = jnp.concatenate([chi, jnp.zeros((1, LANES - cells), F32)], axis=1)
    chi_out[0, :, :] = chi
    chi_in[0, :, :] = chi
    if remote:

        for k in range(1, blocks):
            pltpu.make_async_remote_copy(
                src_ref=chi_out.at[0], dst_ref=chi_in.at[k], send_sem=chi_send_sem.at[0], recv_sem=chi_sem.at[0],
                device_id={"blk": around(k)}, device_id_type=MESH,
            ).start()

    def answer(half):
        slot = slot_rows(half)
        pick = jnp.concatenate([picks[half], picks[half]], axis=0).astype(BF16)

        def gather(t, carry):
            at = pl.ds(pl.multiple_of(t * 8 * TILE, 8 * TILE), 8 * TILE)
            tiles = product(weighted_ref[at, :], pick)
            for k in range(8):
                img_c[half, pl.ds((t * 8 + k) * PITCH, TILE), :] = tiles[k * TILE : (k + 1) * TILE]
            return carry

        def project(q, sums):
            at = pl.ds(q * PITCH, TILE)
            dx = column(q, slot)
            adjoint = img_c[half, at, :]
            over = img_b[half, at, :] * adjoint
            plain = img_a[half, at, :] * adjoint
            moment = over * dy_ref[half, 0]
            second = moment * dy_ref[half, 0]
            plain, over, moment, second = (
                x[0:8] + x[8:16] + (x[16:24] + x[24:32]) for x in (plain, over, moment, second)
            )
            over = over * dx
            return sums[0] + plain, sums[1] + over, sums[2] + moment, sums[3] + (second + over * dx)

        lax.fori_loop(0, 4, gather, 0, unroll=2)
        blur(half, 1, lambda image: half, img_c, img_e, img_c, coef, parts, even_acc)
        sums = lax.fori_loop(0, TILE, project, tuple(jnp.zeros((8, LANES), F32) for _ in range(4)), unroll=4)
        sums = [jnp.sum(s, axis=0, keepdims=True) for s in sums]
        sums[3] = sums[3] - slot(SLOPE) * sums[0]
        back = jnp.concatenate(sums + [slots_ref[half, WEIGHT : WEIGHT + 1, :], jnp.zeros((LANES - 5, LANES), F32)], axis=0).T
        packed = back[0:near]
        for r in range(1, CAP):
            packed = packed + pltpu.roll(back[r * near : (r + 1) * near], r * BACK, 1)
        out_sums[half * near : (half + 1) * near, 0, :] = packed

    answer(1)
    if remote:
        for j in reversed(range(near, peers)):
            send(out_sums.at[j], in_sums.at[j], behind(j), back_send_sem.at[0], back_sem.at[0])
    answer(0)
    if remote:
        for j in reversed(range(1, near)):
            send(out_sums.at[j], in_sums.at[j], behind(j), back_send_sem.at[0], back_sem.at[0])
        in_sums[0] = out_sums[0]
    else:
        in_sums[...] = out_sums[...]

    own_blur(3, 1)
    pairs = [(i, j) for i in range(4) for j in range(i, 4)]

    def gram(p, sums):
        for t in range(TILE // 8):
            at = pl.ds(p * PITCH + t * 8, 8)
            own = [img_d[k, at, :] for k in range(4)]
            sums = tuple(s + own[i] * own[j] for s, (i, j) in zip(sums, pairs))
        return sums

    sums = lax.fori_loop(0, TILE, gram, tuple(jnp.zeros((8, LANES), F32) for _ in pairs))
    for k, s in enumerate(sums):
        gram_ref[k : k + 1, :] = jnp.sum(s, axis=0, keepdims=True)

    if remote:
        await_rows(chi_in, blocks - 1, chi_sem.at[0])
        await_rows(in_sums, peers - 1, back_sem.at[0])

    group = chi_in[0]
    if remote:
        for k in range(1, blocks):
            group = group + chi_in[k]
    group_chi = jnp.sum(group, axis=1, keepdims=True)
    damping = BASE_DAMPING + MISFIT_SCALE * group_chi / pixel_total
    by_rank = dot(in_sums[:, 0, :].T[: CAP * BACK], hits_ref[...])
    rank = rank_ref[...]
    mine = None
    for r in range(CAP):
        part = jnp.where(rank == float(r), by_rank[r * BACK : (r + 1) * BACK], 0.0)
        mine = part if mine is None else mine + part
    extended = jnp.where(flag_ref[...] == 1, 0.0, 1.0)
    per_flux = 1.0 / values_ref[0:1, :]
    scale = [per_flux, 1.0, 1.0, extended]
    weight = mine[4:5]
    gradient = [scale[k] * mine[k : k + 1] for k in range(4)]
    curvature = [[None] * 4 for _ in range(4)]
    for k, (i, j) in enumerate(pairs):
        entry = gram_ref[k : k + 1, :] * (scale[i] * scale[j]) * weight
        curvature[i][j] = entry
        curvature[j][i] = entry
    delta = damped_solve(curvature, gradient, jnp.broadcast_to(damping, (1, LANES)))
    out_ref[...] = jnp.concatenate(delta, axis=0)
    if remote:
        await_rows(out_rows, SIDE - 1, send_sem.at[0])
        await_rows(mid_rows, SIDE - 1, pass_sem.at[0])
        await_rows(out_sums, peers - 1, back_send_sem.at[0])
        await_rows(chi_in, blocks - 1, chi_send_sem.at[0])


def step(bricks, blocks, remote, parameters, sersic, psf_width, point_flag, owner_brick, cell_index, exposure, inv_noise):
    sources, cells = parameters.shape[1], exposure.shape[0]
    vmem = pl.BlockSpec(memory_space=pltpu.VMEM)
    dma = pltpu.SemaphoreType.DMA
    params = dict(vmem_limit_bytes=24 << 20)
    if remote:
        params.update(collective_id=0, has_side_effects=True)
    delta = pl.pallas_call(
        functools.partial(kernel, blocks, blocks * cells * PIXELS, remote),
        out_shape=jax.ShapeDtypeStruct((4, sources), F32),
        in_specs=[pl.BlockSpec(memory_space=pltpu.HBM)] * 8,
        out_specs=vmem,
        scratch_shapes=[
            pltpu.VMEM((4, sources), F32),
            pltpu.VMEM((1, sources), F32),
            pltpu.VMEM((1, sources), F32),
            pltpu.VMEM((1, sources), jnp.int32),
            pltpu.VMEM((1, sources), jnp.int32),
            pltpu.VMEM((1, sources), jnp.int32),
            pltpu.VMEM((cells, PIXELS), F32),
            pltpu.VMEM((1, cells), F32),
            pltpu.VMEM((VALS, LANES), F32),
            pltpu.VMEM((bricks, LANES), F32),
            pltpu.VMEM((1, LANES), F32),
            pltpu.VMEM((2, VALS, LANES), F32),
            pltpu.VMEM((16, LANES), F32),
            pltpu.VMEM((TILE, LANES), F32),
            pltpu.VMEM((2 * TILE, 8, LANES), F32),
            pltpu.VMEM((3, 2, HALF, HALF, 8, LANES), F32),
            pltpu.VMEM((2, HALF, 2, 8, LANES), F32),
            pltpu.VMEM((2, 2, 8, 8, LANES), F32),
            pltpu.VMEM((3, 2, TILE, LANES), F32),
            pltpu.VMEM((2, LINES, LANES), F32),
            pltpu.VMEM((2, LINES, LANES), F32),
            pltpu.VMEM((2, LINES, LANES), F32),
            pltpu.VMEM((4, LINES, LANES), F32),
            pltpu.VMEM((4, LINES, LANES), F32),
            pltpu.VMEM((PIXELS, 2 * cells), F32),
            pltpu.VMEM((PIXELS, 2 * cells), BF16),
            *[pltpu.VMEM((SIDE, SIDE, 1, LANES), F32)] * 3,
            *[pltpu.VMEM((bricks, 1, LANES), F32)] * 2,
            pltpu.VMEM((1, 1, LANES), F32),
            pltpu.VMEM((blocks, 1, LANES), F32),
            dma((8,)),
            *[dma((1,))] * 9,
        ],
        compiler_params=pltpu.CompilerParams(**params),
    )(*[pltpu.with_memory_space_constraint(x, pltpu.HBM) for x in (
        parameters,
        sersic.reshape(1, sources),
        psf_width.reshape(1, sources),
        point_flag.reshape(1, sources),
        owner_brick.reshape(1, sources),
        cell_index.reshape(1, sources),
        exposure,
        inv_noise.reshape(1, cells),
    )])
    return parameters + delta


def solution(mesh):
    bricks, blocks = mesh.shape["brick"], mesh.shape["blk"]
    both = ("brick", "blk")
    in_specs = (P(None, both), P(both), P(both), P(both), P(both, None), P(both), P(both, None), P(both))
    return jax.shard_map(
        functools.partial(step, bricks, blocks, True),
        mesh=mesh, in_specs=in_specs, out_specs=P(None, both), check_vma=False,
    )
```

profile of v0, /device:TPU:6, one launch (start us, length us, event | category | flops | bytes accessed | tf_op | source)
XLA Modules:
  0.0 37.8 jit_solution(14299860863508475986)
XLA Ops:
  0.0 0.0 copy-start
  0.0 37.2 %shard_map.82 = f32[4,128]{1,0:T(4,128)S(1)} custom-call(f32[4,128]{1,0:T(4,128)} %values_hbm.1, f32[1,128]{1,0:T(1,128)} %bitcast.6, f32[1,128]{1,0:T(1,128)} %bitcast.7, s32[1,128]{1,0:T(1,128)} %bitcast.8, s32[1,128]{1,0:T(1,128)} %bitcast.9, s32[1,128]{1,0:T(1,128)} %bitcast.10, f32[32,1024]{1,0:T(8,128)} %exposure_hbm.1, f32[1,32]{1,0:T(1,128)} %bitcast.11), custom_call_target="tpu_custom_call" | custom-call | tf_op jit(solution)/shard_map/pallas_call | solution.py:513
  37.2 0.0 copy-done
  37.3 0.6 %add.3 = f32[4,128]{1,0:T(4,128)} add(f32[4,128]{1,0:T(4,128)S(1)} %copy-done, f32[4,128]{1,0:T(4,128)S(1)} %shard_map.82) | non-fusion elementwise | flops 512 | bytes 6144 | tf_op jit(solution)/shard_map/add | solution.py:563
Async XLA Ops:
  0.0 37.2 %copy-start = (f32[4,128]{1,0:T(4,128)S(1)}, f32[4,128]{1,0:T(4,128)}, u32[]{:S(2)}) copy-start(f32[4,128]{1,0:T(4,128)} %values_hbm.1) | copy-start | bytes 6148
where the time goes:
time: 38 us; the launch traced here: 37.8 us
  Pallas kernels  37.2 us (98%)
  other arithmetic  0.58 us (2%)
    pallas_call x1, Pallas kernels, step(): pl.pallas_call(functools.partial(kernel, blocks, blocks * cells * PIXELS,...  37.2 us

commit v1 on v0

--- a/solution.py
+++ b/solution.py
@@ -27,7 +27,7 @@
 F32 = jnp.float32
 BF16 = jnp.bfloat16
 
-CX, CY, C1, C0, LN, INVN, ITV, NORM, SLOPE, CELL, WEIGHT = range(11)
+CX, CY, C1, C0, LN, LNN, ITV, NORM, SLOPE, CELL, WEIGHT = range(11)
 
 
 def peer_offsets():
@@ -77,7 +77,7 @@
     rows[C1] = jnp.where(is_point, 1.0, 0.5 * inverse_index)
     rows[C0] = jnp.where(is_point, log_itv, jnp.log(bfactor) - log_radius * inverse_index)
     rows[LN] = jnp.where(is_point, math.log(math.pi) - log_itv, log_norm) - jnp.log(ZERO_POINT * flux)
-    rows[INVN] = jnp.where(is_point, 2.0, inverse_index)
+    rows[LNN] = jnp.where(is_point, -math.log(2.0), jnp.log(sersic))
     rows[ITV] = jnp.where(is_point, 1.0e4, inv_two_var)
     rows[NORM] = jnp.where(is_point, 1.0, norm_psf)
     rows[SLOPE] = slope
@@ -95,18 +95,21 @@
     return lax.dot_general(a, b, (((1,), (cb,)), ((), ())), preferred_element_type=F32)
 
 
-def blur_coefficients(row, taps, spread, coef, at):
+def spread_taps(row, taps, spread):
     apart = lax.broadcasted_iota(jnp.int32, (TILE, LANES), 0).astype(F32)
     taps[...] = jnp.exp(-(apart * apart) * row(ITV)) * (0.5 * row(NORM))
     for d in range(TILE):
         value = jnp.broadcast_to(taps[d : d + 1, :], (8, LANES))
         spread[TILE - 1 + d] = value
-        spread[TILE - 1 - d] = value
-    for q in range(HALF):
-        near = spread[TILE - 1 - q : TILE - 1 - q + HALF]
-        far = spread[q : q + HALF]
-        coef[at, 0, q] = near + far
-        coef[at, 1, q] = near - far
+        if d:
+            spread[TILE - 1 - d] = value
+
+
+def blur_column(q, spread, coef, at):
+    near = spread[pl.ds(TILE - 1 - q, HALF)]
+    far = spread[pl.ds(q, HALF)]
+    coef[at, 0, q] = near + far
+    coef[at, 1, q] = near - far
 
 
 def blur_lines(load, store, coef, at, parts, even_acc):
@@ -173,10 +176,11 @@
 def images(q, row, dy_ref, at):
     dx = column(q, row)
     radius_sq = dy_ref[at, 1] + dx * dx
-    power = jnp.exp(row(C1) * jnp.log(radius_sq) + row(C0))
-    image = jnp.exp(-power - row(LN))
-    over = image * (power * row(INVN)) / radius_sq
-    return dx, radius_sq, image, over
+    log_r2 = jnp.log(radius_sq)
+    log_power = row(C1) * log_r2 + row(C0)
+    log_image = -jnp.exp(log_power) - row(LN)
+    over = jnp.exp(log_image + log_power - (log_r2 + row(LNN)))
+    return dx, radius_sq, jnp.exp(log_image), over
 
 
 def damped_solve(curvature, gradient, damping):
@@ -285,19 +289,23 @@
     def row(k):
         return rows_ref[k : k + 1, :]
 
-    blur_coefficients(row, taps, spread, coef, 2)
+    spread_taps(row, taps, spread)
     offsets(row, dy_ref, 2)
 
-    def own_images(q, carry):
-        dx, radius_sq, image, over = images(q, row, dy_ref, 2)
-        at = pl.ds(q * PITCH, TILE)
-        img_d[0, at, :] = image
-        img_d[1, at, :] = over * dx
-        img_d[2, at, :] = over * dy_ref[2, 0]
-        img_d[3, at, :] = over * radius_sq - row(SLOPE) * image
+    def own_images(step, carry):
+        for k in range(8):
+            q = step * 8 + k
+            dx, radius_sq, image, over = images(q, row, dy_ref, 2)
+            at = pl.ds(q * PITCH, TILE)
+            img_d[0, at, :] = image
+            img_d[1, at, :] = over * dx
+            img_d[2, at, :] = over * dy_ref[2, 0]
+            img_d[3, at, :] = over * radius_sq - row(SLOPE) * image
+        for k in range(4):
+            blur_column(step * 4 + k, spread, coef, 2)
         return carry
 
-    lax.fori_loop(0, TILE, own_images, 0, unroll=4)
+    lax.fori_loop(0, TILE // 8, own_images, 0)
 
     def own_blur(first, count):
         blur(first, count, lambda image: 2, img_d, img_e, img_d, coef, parts, even_acc)
@@ -348,17 +356,21 @@
         turned = [received] + [pltpu.roll(received, LANES - r * VALS, 1) for r in range(1, CAP)]
         slots_ref[half] = jnp.concatenate(turned, axis=0).T[:VALS]
         slot = slot_rows(half)
-        blur_coefficients(slot, taps, spread, coef, half)
+        spread_taps(slot, taps, spread)
         offsets(slot, dy_ref, half)
 
-        def slot_images(q, carry):
-            dx, radius_sq, image, over = images(q, slot, dy_ref, half)
-            at = pl.ds(q * PITCH, TILE)
-            img_a[half, at, :] = image
-            img_b[half, at, :] = over
+        def slot_images(step, carry):
+            for k in range(8):
+                q = step * 8 + k
+                dx, radius_sq, image, over = images(q, slot, dy_ref, half)
+                at = pl.ds(q * PITCH, TILE)
+                img_a[half, at, :] = image
+                img_b[half, at, :] = over
+            for k in range(4):
+                blur_column(step * 4 + k, spread, coef, half)
             return carry
 
-        lax.fori_loop(0, TILE, slot_images, 0, unroll=8)
+        lax.fori_loop(0, TILE // 8, slot_images, 0)
         blur(half, 1, lambda image: half, img_a, img_e, img_c, coef, parts, even_acc)
         chosen = jnp.where(cells_at == slot(CELL), 1.0, 0.0)
         picks.append(chosen)

time: 38 us -> 37.8 us (level)
  no operation moved by 1% of the time
where the time goes in v1:
time: 37.8 us; the launch traced here: 37.7 us
  Pallas kernels  37.1 us (98%)
  other arithmetic  0.58 us (2%)
    pallas_call x1, Pallas kernels, step(): pl.pallas_call(functools.partial(kernel, blocks, blocks * cells * PIXELS,...  37.1 us

profile of v1, /device:TPU:6, one launch (start us, length us, event | category | flops | bytes accessed | tf_op | source)
XLA Modules:
  0.0 37.7 jit_solution(13215392567095628810)
XLA Ops:
  0.0 0.0 copy-start
  0.0 37.1 %shard_map.82 = f32[4,128]{1,0:T(4,128)S(1)} custom-call(f32[4,128]{1,0:T(4,128)} %values_hbm.1, f32[1,128]{1,0:T(1,128)} %bitcast.6, f32[1,128]{1,0:T(1,128)} %bitcast.7, s32[1,128]{1,0:T(1,128)} %bitcast.8, s32[1,128]{1,0:T(1,128)} %bitcast.9, s32[1,128]{1,0:T(1,128)} %bitcast.10, f32[32,1024]{1,0:T(8,128)} %exposure_hbm.1, f32[1,32]{1,0:T(1,128)} %bitcast.11), custom_call_target="tpu_custom_call" | custom-call | tf_op jit(solution)/shard_map/pallas_call | solution.py:525
  37.1 0.0 copy-done
  37.1 0.6 %add.3 = f32[4,128]{1,0:T(4,128)} add(f32[4,128]{1,0:T(4,128)S(1)} %copy-done, f32[4,128]{1,0:T(4,128)S(1)} %shard_map.82) | non-fusion elementwise | flops 512 | bytes 6144 | tf_op jit(solution)/shard_map/add | solution.py:575
Async XLA Ops:
  0.0 37.1 %copy-start = (f32[4,128]{1,0:T(4,128)S(1)}, f32[4,128]{1,0:T(4,128)}, u32[]{:S(2)}) copy-start(f32[4,128]{1,0:T(4,128)} %values_hbm.1) | copy-start | bytes 6148

commit v2 on v1

--- a/solution.py
+++ b/solution.py
@@ -18,6 +18,7 @@
 VALS = 32
 BACK = 8
 SIDE = 8
+NEAR_Z = 2
 LANES = 128
 ZERO_POINT = 30.0
 BASE_DAMPING = 0.1
@@ -30,8 +31,22 @@
 CX, CY, C1, C0, LN, LNN, ITV, NORM, SLOPE, CELL, WEIGHT = range(11)
 
 
+def hops(step):
+    return min(step, SIDE - step)
+
+
 def peer_offsets():
-    return [(z, y) for z in sorted(range(SIDE), key=lambda step: (min(step, SIDE - step), step)) for y in range(SIDE)]
+    return [(z, y) for z in sorted(range(SIDE), key=lambda step: (hops(step), step)) for y in range(SIDE)]
+
+
+def slot_peers():
+    def far(j):
+        z, y = (hops(step) for step in peer_offsets()[j])
+        return z + y + (SIDE if z > NEAR_Z else 0)
+
+    ordered = sorted(range(SIDE * SIDE), key=lambda j: (far(j), j))
+    half = len(ordered) // 2
+    return ordered[:half], ordered[half:]
 
 
 def dot(a, b, ca=1, cb=0):
@@ -224,6 +239,37 @@
     out_rows, mid_rows, in_rows, out_sums, in_sums, chi_out, chi_in,
     input_sem, send_sem, mid_sem, pass_sem, near_sem, far_sem, back_send_sem, back_sem, chi_send_sem, chi_sem,
 ):
+    offsets_of = peer_offsets()
+    peers = len(offsets_of)
+    near = peers // 2
+    held = slot_peers()
+    near_z = 2 * NEAR_Z + 1
+    far_first = sorted(range(1, SIDE), key=lambda step: -hops(step))
+    if remote:
+        me = lax.axis_index("brick")
+        lane = lax.axis_index("blk")
+        barrier = pltpu.get_barrier_semaphore()
+        my_z, my_y = me // SIDE, me % SIDE
+        plus_z = [((my_z + k) % SIDE) * SIDE for k in range(SIDE)]
+        plus_y = [(my_y + k) % SIDE for k in range(SIDE)]
+
+        def ahead(j):
+            return plus_z[offsets_of[j][0]] + plus_y[offsets_of[j][1]]
+
+        def behind(j):
+            return plus_z[-offsets_of[j][0] % SIDE] + plus_y[-offsets_of[j][1] % SIDE]
+
+        def around(k):
+            return jnp.where(lane + k >= blocks, lane + k - blocks, lane + k)
+
+        for k in far_first:
+            pl.semaphore_signal(barrier, inc=1, device_id={"brick": ahead(k)}, device_id_type=MESH)
+        for k in reversed(range(1, SIDE)):
+            pl.semaphore_signal(barrier, inc=1, device_id={"brick": ahead(k * SIDE)}, device_id_type=MESH)
+        for k in range(1, blocks):
+            pl.semaphore_signal(barrier, inc=1, device_id={"blk": around(k)}, device_id_type=MESH)
+    else:
+        my_z, my_y = 0, 0
     inputs = [
         pltpu.make_async_copy(source, target, input_sem.at[k])
         for k, (source, target) in enumerate(
@@ -241,33 +287,6 @@
     ]
     for copy in inputs:
         copy.start()
-    offsets_of = peer_offsets()
-    peers = len(offsets_of)
-    near = peers // 2
-    if remote:
-        me = lax.axis_index("brick")
-        lane = lax.axis_index("blk")
-        barrier = pltpu.get_barrier_semaphore()
-        my_z, my_y = me // SIDE, me % SIDE
-        plus_z = [((my_z + k) % SIDE) * SIDE for k in range(SIDE)]
-        plus_y = [(my_y + k) % SIDE for k in range(SIDE)]
-
-        def ahead(j):
-            return plus_z[offsets_of[j][0]] + plus_y[offsets_of[j][1]]
-
-        def behind(j):
-            return plus_z[-offsets_of[j][0] % SIDE] + plus_y[-offsets_of[j][1] % SIDE]
-
-        def around(k):
-            return jnp.where(lane + k >= blocks, lane + k - blocks, lane + k)
-
-        for k in reversed(range(1, SIDE)):
-            pl.semaphore_signal(barrier, inc=1, device_id={"brick": ahead(k)}, device_id_type=MESH)
-            pl.semaphore_signal(barrier, inc=1, device_id={"brick": ahead(k * SIDE)}, device_id_type=MESH)
-        for k in range(1, blocks):
-            pl.semaphore_signal(barrier, inc=1, device_id={"blk": around(k)}, device_id_type=MESH)
-    else:
-        my_z, my_y = 0, 0
     for copy in inputs[:6]:
         copy.wait()
 
@@ -322,14 +341,14 @@
         def await_rows(ref, count, sem):
             pltpu.make_async_copy(ref.at[0:count], ref.at[0:count], sem).wait()
 
-        for k in range(1, SIDE):
+        for k in far_first:
             send(out_rows.at[:, k], mid_rows.at[:, k], ahead(k), send_sem.at[0], mid_sem.at[0])
     mid_rows[:, 0] = out_rows[:, 0]
     own_blur(0, 2)
     if remote:
         await_rows(mid_rows, SIDE - 1, mid_sem.at[0])
         for k in reversed(range(1, SIDE)):
-            landed = (near_sem if k < SIDE // 2 else far_sem).at[0]
+            landed = (near_sem if k < near_z else far_sem).at[0]
             send(mid_rows.at[k], in_rows.at[k], ahead(k * SIDE), pass_sem.at[0], landed)
         in_rows[0] = mid_rows[0]
     else:
@@ -352,7 +371,7 @@
         return lambda k: slots_ref[half, k : k + 1, :]
 
     def render(half):
-        received = in_rows[half * SIDE // 2 : (half + 1) * SIDE // 2, :, 0, :].reshape(near, LANES)
+        received = jnp.concatenate([in_rows[j // SIDE, j % SIDE] for j in held[half]], axis=0)
         turned = [received] + [pltpu.roll(received, LANES - r * VALS, 1) for r in range(1, CAP)]
         slots_ref[half] = jnp.concatenate(turned, axis=0).T[:VALS]
         slot = slot_rows(half)
@@ -388,11 +407,11 @@
         return carry
 
     if remote:
-        await_rows(in_rows, SIDE // 2 - 1, near_sem.at[0])
+        await_rows(in_rows, near_z - 1, near_sem.at[0])
     render(0)
     lax.fori_loop(0, 4, subtract_near, 0, unroll=2)
     if remote:
-        await_rows(in_rows, SIDE // 2, far_sem.at[0])
+        await_rows(in_rows, SIDE - near_z, far_sem.at[0])
     render(1)
     weights_twice = jnp.concatenate([weights, weights], axis=1)
     is_high = lax.broadcasted_iota(jnp.int32, (1, 2 * cells), 1) < cells
@@ -454,17 +473,23 @@
             packed = packed + pltpu.roll(back[r * near : (r + 1) * near], r * BACK, 1)
         out_sums[half * near : (half + 1) * near, 0, :] = packed
 
+    def send_answers(half):
+        for k in reversed(range(near)):
+            j = held[half][k]
+            if j:
+                send(out_sums.at[half * near + k], in_sums.at[j], behind(j), back_send_sem.at[0], back_sem.at[0])
+
     answer(1)
     if remote:
-        for j in reversed(range(near, peers)):
-            send(out_sums.at[j], in_sums.at[j], behind(j), back_send_sem.at[0], back_sem.at[0])
+        send_answers(1)
     answer(0)
     if remote:
-        for j in reversed(range(1, near)):
-            send(out_sums.at[j], in_sums.at[j], behind(j), back_send_sem.at[0], back_sem.at[0])
+        send_answers(0)
         in_sums[0] = out_sums[0]
     else:
-        in_sums[...] = out_sums[...]
+        for half in range(2):
+            for k in range(near):
+                in_sums[held[half][k]] = out_sums[half * near + k]
 
     own_blur(3, 1)
     pairs = [(i, j) for i in range(4) for j in range(i, 4)]

time: 37.8 us -> 36.7 us (0.971)
  Pallas kernels: 37.1 us -> 36 us
    pallas_call x1, Pallas kernels: 37.1 us -> 36 us  [step(): pl.pallas_call(functools.partial(kernel, blocks, blocks * cells * PIXELS,...]
where the time goes in v2:
time: 36.7 us; the launch traced here: 36.6 us
  Pallas kernels  36 us (98%)
  other arithmetic  0.58 us (2%)
    pallas_call x1, Pallas kernels, step(): pl.pallas_call(functools.partial(kernel, blocks, blocks * cells * PIXELS,...  36 us

profile of v2, /device:TPU:6, one launch (start us, length us, event | category | flops | bytes accessed | tf_op | source)
XLA Modules:
  0.0 36.6 jit_solution(809739387907606615)
XLA Ops:
  0.0 0.0 copy-start
  0.0 36.0 %shard_map.82 = f32[4,128]{1,0:T(4,128)S(1)} custom-call(f32[4,128]{1,0:T(4,128)} %values_hbm.1, f32[1,128]{1,0:T(1,128)} %bitcast.6, f32[1,128]{1,0:T(1,128)} %bitcast.7, s32[1,128]{1,0:T(1,128)} %bitcast.8, s32[1,128]{1,0:T(1,128)} %bitcast.9, s32[1,128]{1,0:T(1,128)} %bitcast.10, f32[32,1024]{1,0:T(8,128)} %exposure_hbm.1, f32[1,32]{1,0:T(1,128)} %bitcast.11), custom_call_target="tpu_custom_call" | custom-call | tf_op jit(solution)/shard_map/pallas_call | solution.py:550
  36.0 0.0 copy-done
  36.0 0.6 %add.3 = f32[4,128]{1,0:T(4,128)} add(f32[4,128]{1,0:T(4,128)S(1)} %copy-done, f32[4,128]{1,0:T(4,128)S(1)} %shard_map.82) | non-fusion elementwise | flops 512 | bytes 6144 | tf_op jit(solution)/shard_map/add | solution.py:600
Async XLA Ops:
  0.0 36.0 %copy-start = (f32[4,128]{1,0:T(4,128)S(1)}, f32[4,128]{1,0:T(4,128)}, u32[]{:S(2)}) copy-start(f32[4,128]{1,0:T(4,128)} %values_hbm.1) | copy-start | bytes 6148

commit v3 on v2

--- a/solution.py
+++ b/solution.py
@@ -149,32 +149,40 @@
 
 
 def blur(first, count, at_of, src, mid, dst, coef, parts, even_acc):
-    def along_major(step, carry):
-        image, start = first + step // 2, (step % 2) * 16
-
-        def load(q):
-            return src[image, pl.ds(q * PITCH + start, 16), :].reshape(2, 8, LANES)
-
-        def store(q, value):
-            mid[image, pl.ds(q * PITCH + start, 16), :] = value.reshape(16, LANES)
-
-        blur_lines(load, store, coef, at_of(image), parts, even_acc)
+    def along_major(k, carry):
+        image = first + k
+        for part in range(2):
+            start = part * 16
+
+            def load(q, start=start):
+                return src[image, pl.ds(q * PITCH + start, 16), :].reshape(2, 8, LANES)
+
+            def store(q, value, start=start):
+                mid[image, pl.ds(q * PITCH + start, 16), :] = value.reshape(16, LANES)
+
+            blur_lines(load, store, coef, at_of(image), parts.at[part], even_acc.at[part])
         return carry
 
-    def along_minor(step, carry):
-        image, start = first + step // 2, (step % 2) * 16
-
-        def load(p):
-            return mid[image, pl.ds(start * PITCH + p, 16, stride=PITCH), :].reshape(2, 8, LANES)
-
-        def store(p, value):
-            dst[image, pl.ds(p * PITCH + start, 16), :] = value.reshape(16, LANES)
-
-        blur_lines(load, store, coef, at_of(image), parts, even_acc)
+    def along_minor(k, carry):
+        image = first + k
+        for part in range(2):
+            start = part * 16
+
+            def load(p, start=start):
+                return mid[image, pl.ds(start * PITCH + p, 16, stride=PITCH), :].reshape(2, 8, LANES)
+
+            def store(p, value, start=start):
+                dst[image, pl.ds(p * PITCH + start, 16), :] = value.reshape(16, LANES)
+
+            blur_lines(load, store, coef, at_of(image), parts.at[part], even_acc.at[part])
         return carry
 
-    lax.fori_loop(0, 2 * count, along_major, 0)
-    lax.fori_loop(0, 2 * count, along_minor, 0)
+    if count == 1:
+        along_major(0, 0)
+        along_minor(0, 0)
+    else:
+        lax.fori_loop(0, count, along_major, 0)
+        lax.fori_loop(0, count, along_minor, 0)
 
 
 def offsets(row, dy_ref, at):
@@ -409,7 +417,7 @@
     if remote:
         await_rows(in_rows, near_z - 1, near_sem.at[0])
     render(0)
-    lax.fori_loop(0, 4, subtract_near, 0, unroll=2)
+    lax.fori_loop(0, 4, subtract_near, 0, unroll=4)
     if remote:
         await_rows(in_rows, SIDE - near_z, far_sem.at[0])
     render(1)
@@ -424,7 +432,7 @@
         weighted_ref[at, :] = jnp.where(is_high, high, weighted - high).astype(BF16)
         return chi + jnp.sum((weighted * misfit).reshape(TILE, 8, 2 * cells), axis=0)
 
-    chi = lax.fori_loop(0, 4, residual, jnp.zeros((8, 2 * cells), F32), unroll=2)
+    chi = lax.fori_loop(0, 4, residual, jnp.zeros((8, 2 * cells), F32), unroll=4)
     chi = jnp.sum(chi, axis=0, keepdims=True)[:, :cells]
     chi = jnp.concatenate([chi, jnp.zeros((1, LANES - cells), F32)], axis=1)
     chi_out[0, :, :] = chi
@@ -462,9 +470,9 @@
             over = over * dx
             return sums[0] + plain, sums[1] + over, sums[2] + moment, sums[3] + (second + over * dx)
 
-        lax.fori_loop(0, 4, gather, 0, unroll=2)
+        lax.fori_loop(0, 4, gather, 0, unroll=4)
         blur(half, 1, lambda image: half, img_c, img_e, img_c, coef, parts, even_acc)
-        sums = lax.fori_loop(0, TILE, project, tuple(jnp.zeros((8, LANES), F32) for _ in range(4)), unroll=4)
+        sums = lax.fori_loop(0, TILE, project, tuple(jnp.zeros((8, LANES), F32) for _ in range(4)), unroll=8)
         sums = [jnp.sum(s, axis=0, keepdims=True) for s in sums]
         sums[3] = sums[3] - slot(SLOPE) * sums[0]
         back = jnp.concatenate(sums + [slots_ref[half, WEIGHT : WEIGHT + 1, :], jnp.zeros((LANES - 5, LANES), F32)], axis=0).T
@@ -569,8 +577,8 @@
             pltpu.VMEM((TILE, LANES), F32),
             pltpu.VMEM((2 * TILE, 8, LANES), F32),
             pltpu.VMEM((3, 2, HALF, HALF, 8, LANES), F32),
-            pltpu.VMEM((2, HALF, 2, 8, LANES), F32),
-            pltpu.VMEM((2, 2, 8, 8, LANES), F32),
+            pltpu.VMEM((2, 2, HALF, 2, 8, LANES), F32),
+            pltpu.VMEM((2, 2, 2, 8, 8, LANES), F32),
             pltpu.VMEM((3, 2, TILE, LANES), F32),
             pltpu.VMEM((2, LINES, LANES), F32),
             pltpu.VMEM((2, LINES, LANES), F32),

time: 36.7 us -> 36.2 us (0.986)
  Pallas kernels: 36 us -> 35.5 us
    pallas_call x1, Pallas kernels: 36 us -> 35.5 us  [step(): pl.pallas_call(functools.partial(kernel, blocks, blocks * cells * PIXELS,...]
where the time goes in v3:
time: 36.2 us; the launch traced here: 36.1 us
  Pallas kernels  35.5 us (98%)
  other arithmetic  0.58 us (2%)
    pallas_call x1, Pallas kernels, step(): pl.pallas_call(functools.partial(kernel, blocks, blocks * cells * PIXELS,...  35.5 us

profile of v3, /device:TPU:6, one launch (start us, length us, event | category | flops | bytes accessed | tf_op | source)
XLA Modules:
  0.0 36.1 jit_solution(7020704311840889651)
XLA Ops:
  0.0 0.0 copy-start
  0.0 35.5 %shard_map.82 = f32[4,128]{1,0:T(4,128)S(1)} custom-call(f32[4,128]{1,0:T(4,128)} %values_hbm.1, f32[1,128]{1,0:T(1,128)} %bitcast.6, f32[1,128]{1,0:T(1,128)} %bitcast.7, s32[1,128]{1,0:T(1,128)} %bitcast.8, s32[1,128]{1,0:T(1,128)} %bitcast.9, s32[1,128]{1,0:T(1,128)} %bitcast.10, f32[32,1024]{1,0:T(8,128)} %exposure_hbm.1, f32[1,32]{1,0:T(1,128)} %bitcast.11), custom_call_target="tpu_custom_call" | custom-call | tf_op jit(solution)/shard_map/pallas_call | solution.py:558
  35.5 0.0 copy-done
  35.5 0.6 %add.3 = f32[4,128]{1,0:T(4,128)} add(f32[4,128]{1,0:T(4,128)S(1)} %copy-done, f32[4,128]{1,0:T(4,128)S(1)} %shard_map.82) | non-fusion elementwise | flops 512 | bytes 6144 | tf_op jit(solution)/shard_map/add | solution.py:608
Async XLA Ops:
  0.0 35.5 %copy-start = (f32[4,128]{1,0:T(4,128)S(1)}, f32[4,128]{1,0:T(4,128)}, u32[]{:S(2)}) copy-start(f32[4,128]{1,0:T(4,128)} %values_hbm.1) | copy-start | bytes 6148

commit v4 on v3

--- a/solution.py
+++ b/solution.py
@@ -397,7 +397,7 @@
                 blur_column(step * 4 + k, spread, coef, half)
             return carry
 
-        lax.fori_loop(0, TILE // 8, slot_images, 0)
+        lax.fori_loop(0, TILE // 8, slot_images, 0, unroll=4)
         blur(half, 1, lambda image: half, img_a, img_e, img_c, coef, parts, even_acc)
         chosen = jnp.where(cells_at == slot(CELL), 1.0, 0.0)
         picks.append(chosen)
@@ -433,18 +433,6 @@
         return chi + jnp.sum((weighted * misfit).reshape(TILE, 8, 2 * cells), axis=0)
 
     chi = lax.fori_loop(0, 4, residual, jnp.zeros((8, 2 * cells), F32), unroll=4)
-    chi = jnp.sum(chi, axis=0, keepdims=True)[:, :cells]
-    chi = jnp.concatenate([chi, jnp.zeros((1, LANES - cells), F32)], axis=1)
-    chi_out[0, :, :] = chi
-    chi_in[0, :, :] = chi
-    if remote:
-
-        for k in range(1, blocks):
-            pltpu.make_async_remote_copy(
-                src_ref=chi_out.at[0], dst_ref=chi_in.at[k], send_sem=chi_send_sem.at[0], recv_sem=chi_sem.at[0],
-                device_id={"blk": around(k)}, device_id_type=MESH,
-            ).start()
-
     def answer(half):
         slot = slot_rows(half)
         pick = jnp.concatenate([picks[half], picks[half]], axis=0).astype(BF16)
@@ -472,7 +460,7 @@
 
         lax.fori_loop(0, 4, gather, 0, unroll=4)
         blur(half, 1, lambda image: half, img_c, img_e, img_c, coef, parts, even_acc)
-        sums = lax.fori_loop(0, TILE, project, tuple(jnp.zeros((8, LANES), F32) for _ in range(4)), unroll=8)
+        sums = lax.fori_loop(0, TILE, project, tuple(jnp.zeros((8, LANES), F32) for _ in range(4)), unroll=16)
         sums = [jnp.sum(s, axis=0, keepdims=True) for s in sums]
         sums[3] = sums[3] - slot(SLOPE) * sums[0]
         back = jnp.concatenate(sums + [slots_ref[half, WEIGHT : WEIGHT + 1, :], jnp.zeros((LANES - 5, LANES), F32)], axis=0).T
@@ -490,6 +478,17 @@
     answer(1)
     if remote:
         send_answers(1)
+    chi = jnp.sum(chi, axis=0, keepdims=True)[:, :cells]
+    chi = jnp.concatenate([chi, jnp.zeros((1, LANES - cells), F32)], axis=1)
+    chi_out[0, :, :] = chi
+    chi_in[0, :, :] = chi
+    if remote:
+
+        for k in range(1, blocks):
+            pltpu.make_async_remote_copy(
+                src_ref=chi_out.at[0], dst_ref=chi_in.at[k], send_sem=chi_send_sem.at[0], recv_sem=chi_sem.at[0],
+                device_id={"blk": around(k)}, device_id_type=MESH,
+            ).start()
     answer(0)
     if remote:
         send_answers(0)
@@ -552,7 +551,7 @@
     sources, cells = parameters.shape[1], exposure.shape[0]
     vmem = pl.BlockSpec(memory_space=pltpu.VMEM)
     dma = pltpu.SemaphoreType.DMA
-    params = dict(vmem_limit_bytes=24 << 20)
+    params = dict(vmem_limit_bytes=36 << 20)
     if remote:
         params.update(collective_id=0, has_side_effects=True)
     delta = pl.pallas_call(

time: 36.2 us -> 36 us (level)
  no operation moved by 1% of the time
where the time goes in v4:
time: 36 us; the launch traced here: 35.9 us
  Pallas kernels  35.3 us (98%)
  other arithmetic  0.58 us (2%)
    pallas_call x1, Pallas kernels, step(): pl.pallas_call(functools.partial(kernel, blocks, blocks * cells * PIXELS,...  35.3 us

profile of v4, /device:TPU:6, one launch (start us, length us, event | category | flops | bytes accessed | tf_op | source)
XLA Modules:
  0.0 35.9 jit_solution(1666943561870176480)
XLA Ops:
  0.0 0.0 copy-start
  0.0 35.3 %shard_map.82 = f32[4,128]{1,0:T(4,128)S(1)} custom-call(f32[4,128]{1,0:T(4,128)} %values_hbm.1, f32[1,128]{1,0:T(1,128)} %bitcast.6, f32[1,128]{1,0:T(1,128)} %bitcast.7, s32[1,128]{1,0:T(1,128)} %bitcast.8, s32[1,128]{1,0:T(1,128)} %bitcast.9, s32[1,128]{1,0:T(1,128)} %bitcast.10, f32[32,1024]{1,0:T(8,128)} %exposure_hbm.1, f32[1,32]{1,0:T(1,128)} %bitcast.11), custom_call_target="tpu_custom_call" | custom-call | tf_op jit(solution)/shard_map/pallas_call | solution.py:557
  35.3 0.0 copy-done
  35.3 0.6 %add.3 = f32[4,128]{1,0:T(4,128)} add(f32[4,128]{1,0:T(4,128)S(1)} %copy-done, f32[4,128]{1,0:T(4,128)S(1)} %shard_map.82) | non-fusion elementwise | flops 512 | bytes 6144 | tf_op jit(solution)/shard_map/add | solution.py:607
Async XLA Ops:
  0.0 35.3 %copy-start = (f32[4,128]{1,0:T(4,128)S(1)}, f32[4,128]{1,0:T(4,128)}, u32[]{:S(2)}) copy-start(f32[4,128]{1,0:T(4,128)} %values_hbm.1) | copy-start | bytes 6148
